TPU v7x, 32 devices: a whole 2x2x4 slice. The times are simulated.
32 devices in a mesh: groups: 2 (over x), tile: 16 (over z, y, core).
Axes of the slice: x: 2, y: 2, z: 4, core: 2. Of those that a mesh axis runs over, the one named last changes fastest.
Arguments:
- tracer_state: float32 [2, 50, 4096], P(None, None, ('groups', 'tile')), parts along dimension 2, may hold values from -6 to 6
- krylov_direction: float32 [2, 50, 4096], P(None, None, ('groups', 'tile')), parts along dimension 2, may hold values from -6 to 6
- explicit_tiles: bfloat16 [800, 6, 128, 128], P('tile')
- implicit_tiles: bfloat16 [800, 3, 128, 128], P('tile')
- explicit_columns: int32 [800, 6], P('tile'), may hold values from 0 to 450, as said below
- ghost_levels: int32 [256, 25], P('tile'), may hold values from 0 to 50, as said below
- wet_levels: int32 [2048], P('tile'), may hold values from 0 to 50
- surface_light: float32 [4096], P(('groups', 'tile')), parts along dimension 0, may hold values from 0.25 to 4
- martin_exponent: float32 [4096], P(('groups', 'tile')), parts along dimension 0, may hold values from 0.5 to 2
- column_slots: int32 [256, 12], P('tile'), may hold values from 0 to 128, as said below
Outputs:
- state_out: float32 [2, 50, 4096], P(None, None, ('groups', 'tile')), parts along dimension 2
- tangent_out: float32 [2, 50, 4096], P(None, None, ('groups', 'tile')), parts along dimension 2
- export_flux: float32 [6144], P(('groups', 'tile')), parts along dimension 0
There are 2 independent parts, one for each index of `groups`. A program takes and returns all parts, laid end to end along the dimension named above; an argument that names none is the same for every part. Nothing has to cross between parts.
Inputs may be any that keep to these rules, and one draw needn't show every extreme that they name: `explicit_columns`: row d * 50 + l holds l, then l - 1 and l + 1 (50 beyond the ends), then one position for each of the devices d - 1, d + 1 and d + D / 2 of the D devices (wrapping), in that order: 51 + s * 25 + l when ghost_levels sends level l from that device s to d, else 50. `ghost_levels`: row s * D + d, slot k, holds k or 50. It holds k exactly for k below a depth of 1 to 25 when s is d - 1, d + 1 or d + D / 2 (wrapping), and 50 for all other pairs; some device gets depth 25 from all three. `column_slots`: row s * D + b lists local columns of device s handed to device b, 128 marking an empty slot. Each column of s with wet_levels above 0 stands exactly once in rows s * D to s * D + D - 1, no dry column does, and some row is full.
All inputs are finite; a program needn't handle non-finite values.
Results may differ from a plain program's by a relative error of at most 0.012.
Values may be sent and summed in bfloat16 or wider, within the bound.
A program may use at most 64 MiB of HBM per device.

v0:
```python
import jax
import jax.numpy as jnp
from jax import lax
from jax.sharding import PartitionSpec as P

EUPHOTIC = 6
STEPS = 3


max_uptake = 1.0
half_saturation = 0.5
dop_fraction = 0.67
dop_decay = 0.2
time_step = 0.5


def shifted(value, axis, steps):
    count = lax.axis_size(axis)
    pairs = [(source, (source + steps) % count) for source in range(count)]
    return lax.ppermute(value, axis, pairs)


def sources(phosphate, organic, depth_count, surface_light, martin_exponent):
    levels = jnp.arange(phosphate.shape[0], dtype=jnp.float32)[:, None]
    wet_mask = (levels < depth_count[None, :]).astype(jnp.float32)
    sunlit = (levels < EUPHOTIC).astype(jnp.float32)
    depth_ratio = (levels + 1.0) ** 1.5 / (EUPHOTIC * 1.0) ** 1.5
    reaching = jnp.where(
        levels >= EUPHOTIC - 1, jnp.exp(-martin_exponent[None, :] * jnp.log(depth_ratio)), 1.0
    )
    passing = reaching * (levels < depth_count[None, :] - 1.0).astype(jnp.float32)
    passing_above = jnp.concatenate([jnp.ones_like(passing[:1]), passing[:-1]], 0)
    squared = phosphate * phosphate
    uptake = (
        max_uptake
        * surface_light[None, :]
        * jnp.exp(-2.0 * levels / EUPHOTIC)
        * sunlit
        * wet_mask
        * squared
        / (half_saturation**2 + squared)
    )
    export = (1.0 - dop_fraction) * jnp.sum(uptake, 0)
    remineral = export[None, :] * (passing_above - passing)
    decayed = dop_decay * organic * wet_mask
    return (-uptake + decayed + remineral, dop_fraction * uptake - decayed, export)


def column_sources(columns, params):

    def column_rates(phosphate, organic):
        return sources(phosphate, organic, params[0], params[1], params[2])

    primal, tangent = jax.jvp(
        column_rates, (columns[:, 0], columns[:, 1]), (columns[:, 2], columns[:, 3])
    )
    return (jnp.stack([primal[0], primal[1], tangent[0], tangent[1]], 1), primal[2])


def fetch_ghosts(outgoing):
    tile_count = lax.axis_size("tile")
    my_index = lax.axis_index("tile")
    arrived = jnp.zeros_like(outgoing)
    for offset in (1, -1, tile_count // 2):
        sending = lax.dynamic_slice_in_dim(outgoing, (my_index + offset) % tile_count, 1, 0)
        incoming = shifted(sending, "tile", offset)
        arrived = lax.dynamic_update_slice_in_dim(
            arrived, incoming, (my_index - offset) % tile_count, 0
        )
    return arrived


def on_device(
    tracer_state,
    krylov_direction,
    explicit_tiles,
    implicit_tiles,
    explicit_columns,
    ghost_levels,
    wet_levels,
    surface_light,
    martin_exponent,
    column_slots,
):
    levels = tracer_state.shape[1]
    column_count = tracer_state.shape[2]
    half_channels = tracer_state.shape[0]
    channels = 2 * half_channels
    depth_count = wet_levels.astype(jnp.float32)
    params = jnp.stack([depth_count, surface_light, martin_exponent])
    wet_mask = (jnp.arange(levels, dtype=jnp.float32)[:, None] < depth_count[None, :]).astype(
        jnp.float32
    )
    fields = jnp.concatenate([tracer_state, krylov_direction], 0).transpose(1, 0, 2)
    export_total = jnp.zeros((column_count,), jnp.float32)
    boundary = jnp.zeros((1, channels, column_count), jnp.bfloat16)
    for time_index in range(STEPS):
        source_rates, export = column_sources(fields, params)
        export_total = export_total + export
        rounded = jnp.concatenate([fields.astype(jnp.bfloat16), boundary], 0)
        ghosts = fetch_ghosts(rounded[ghost_levels])
        tile_pool = jnp.concatenate([rounded, ghosts.reshape(-1, channels, column_count)], 0)
        carried = jnp.einsum(
            "lkcj,lkji->lci",
            tile_pool[explicit_columns],
            explicit_tiles,
            preferred_element_type=jnp.float32,
        )
        intermediate = (carried + time_step * source_rates).astype(jnp.bfloat16)
        padded_field = jnp.concatenate([boundary, intermediate, boundary], 0)
        stacked = jnp.stack([padded_field[:-2], padded_field[1:-1], padded_field[2:]], 1)
        settled = jnp.einsum(
            "lkcj,lkji->lci", stacked, implicit_tiles, preferred_element_type=jnp.float32
        )
        fields = wet_mask[:, None, :] * settled
    slot_values = jnp.concatenate([export_total, jnp.zeros((1,), jnp.float32)])[column_slots]
    export_flux = lax.all_to_all(
        slot_values, "tile", split_axis=0, concat_axis=0, tiled=True
    ).reshape(-1)
    result = fields.transpose(1, 0, 2)
    return (result[:half_channels], result[half_channels:], export_flux)


def solution(mesh):
    return jax.shard_map(
        on_device,
        mesh=mesh,
        in_specs=(
            P(None, None, ("groups", "tile")),
            P(None, None, ("groups", "tile")),
            P("tile", None, None, None),
            P("tile", None, None, None),
            P("tile", None),
            P("tile", None),
            P("tile"),
            P(("groups", "tile")),
            P(("groups", "tile")),
            P("tile", None),
        ),
        out_specs=(
            P(None, None, ("groups", "tile")),
            P(None, None, ("groups", "tile")),
            P(("groups", "tile")),
        ),
        check_vma=False,
    )
```

profile of v0, /device:TPU:0, one launch (start us, length us, event | category | flops | bytes accessed | tf_op | source)
XLA Modules:
  0.0 86.5 jit_solution(18425667601931482971)
XLA Ops:
  0.7 0.8 copy.92
  1.5 0.8 copy.93
  2.3 0.7 compare_select_fusion.1
  3.0 0.1 reshape.331
  3.2 2.1 %gather_fusion = bf16[400,4,128]{2,1,0:T(4,128)(2,1)S(1)} fusion(bf16[51,4,128]{2,1,0:T(4,128)(2,1)S(1)} %concatenate.54.clone, s32[1024]{0:T(1024)S(1)} %pad_clamp_fusion.2), kind=kCustom, calls=%fused_computation | custom fusion | bytes 820800 | tf_op jit(solution)/shard_map/gather | solution.py:101
  5.4 0.5 collective-permute-start
  5.9 5.0 %collective-permute-start.1 = (bf16[1,25,4,128]{3,2,1,0:T(4,128)(2,1)S(1)}, bf16[1,25,4,128]{3,2,1,0:T(4,128)(2,1)S(1)}, u32[]{:S(2)}, u32[]{:S(2)}) collective-permute-start(bf16[1,25,4,128]{3,2,1,0:T(4,128)(2,1)S(1)} %get-tuple-element.33), channel_id=1, source_target_pairs={{0,15},{1,0},{2,1},{3,2},{4,3},{5,4},{6,5},{7,6},{8,7},{9,8},{10,9... | collective-permute-start | bytes 76808 | tf_op jit(solution)/shard_map/ppermute | solution.py:20
  10.9 1.2 %collective-permute-start.2 = (bf16[1,25,4,128]{3,2,1,0:T(4,128)(2,1)S(1)}, bf16[1,25,4,128]{3,2,1,0:T(4,128)(2,1)S(1)}, u32[]{:S(2)}, u32[]{:S(2)}) collective-permute-start(bf16[1,25,4,128]{3,2,1,0:T(4,128)(2,1)S(1)} %get-tuple-element.32), channel_id=1, source_target_pairs={{0,8},{1,9},{2,10},{3,11},{4,12},{5,13},{6,14},{7,15},{8,0},{9,1},... | collective-permute-start | bytes 76808 | tf_op jit(solution)/shard_map/ppermute | solution.py:20
  12.2 0.7 convert_element_type.46
  12.8 0.7 broadcast_add_fusion
  13.5 0.8 fusion.85
  14.3 0.8 select_subtract_fusion.3
  15.1 0.7 neg.43
  15.7 0.7 compare_select_fusion.2
  16.4 0.1 copy.96
  16.5 0.1 reshape.339
  16.7 0.7 compare_select_fusion
  17.4 0.1 reshape.379
  17.5 0.1 select_select_fusion
  17.6 0.8 fusion.63
  18.4 0.1 pad.40.clone
  18.5 0.1 broadcast.361.clone
  18.7 2.6 %pad_maximum_fusion = bf16[451,4,128]{2,1,0:T(4,128)(2,1)S(1)} fusion(bf16[400,4,128]{2,1,0:T(4,128)(2,1)S(1)} %bitcast.225, bf16[50,4,128]{2,1,0:T(4,128)(2,1)S(1)} %copy.95, bf16[451]{0:T(512)(128)(2,1)S(1)} %pad.40.clone), kind=kLoop, calls=%fused_computation.21 | loop fusion | flops 461824 | bytes 923526 | tf_op jit(solution)/shard_map/concatenate | solution.py:102
  21.3 2.2 %gather_fusion.1 = bf16[300,4,128]{2,1,0:T(4,128)(2,1)S(1)} fusion(bf16[451,4,128]{2,1,0:T(4,128)(2,1)S(1)} %pad_maximum_fusion, s32[1024]{0:T(1024)S(1)} %pad_clamp_fusion.1), kind=kCustom, calls=%fused_computation.1 | custom fusion | bytes 615600 | tf_op jit(solution)/shard_map/gather | solution.py:105
  23.6 5.4 %fusion.12 = bf16[50,4,128]{2,1,0:T(4,128)(2,1)S(1)} fusion(bf16[50,6,4,128]{3,2,1,0:T(4,128)(2,1)S(1)} %bitcast.222, bf16[50,6,128,128]{3,2,1,0:T(8,128)(2,1)} %param.12, f32[50,4,128]{2,0,1:T(8,128)S(1)} %pad_maximum_fusion.4), kind=kOutput, calls=%fused_computation.19 | convolution fusion | flops 39398400 | bytes 10291200 | tf_op jit(solution)/shard_map/lkcj,lkji->lci/dot_general | solution.py:103
  29.1 1.0 %fusion.4 = f32[50,4,128]{2,1,0:T(4,128)S(1)} fusion(bf16[50,3,128,128]{3,2,1,0:T(8,128)(2,1)S(1)} %bitcast.216, bf16[50,1,4,128]{3,2,0,1:T(4,128)(2,1)S(1)} %get-tuple-element.58, bf16[50,1,4,128]{3,2,0,1:T(4,128)(2,1)S(1)} %bitcast.234, bf16[50,1,4,128]{3,2,0,1:T(4,128)(2,1)S(1)} %get-tuple-element.57), kind=kOutput, calls=%fused_computation.11 | convolution fusion | flops 20121600 | bytes 5171200 | tf_op jit(solution)/shard_map/lkcj,lkji->lci/dot_general | solution.py:112
  30.1 2.1 %gather_fusion.2 = bf16[400,4,128]{2,1,0:T(4,128)(2,1)S(1)} fusion(bf16[51,4,128]{2,1,0:T(4,128)(2,1)S(1)} %concatenate.59.clone, s32[1024]{0:T(1024)S(1)} %pad_clamp_fusion.2), kind=kCustom, calls=%fused_computation.2 | custom fusion | bytes 820800 | tf_op jit(solution)/shard_map/gather | solution.py:101
  32.3 0.1 collective-permute-start.3
  32.4 0.1 fusion.83
  32.5 0.1 fusion.53
  32.6 0.1 select_subtract_fusion.1
  32.7 4.7 %collective-permute-start.4 = (bf16[1,25,4,128]{3,2,1,0:T(4,128)(2,1)S(1)}, bf16[1,25,4,128]{3,2,1,0:T(4,128)(2,1)S(1)}, u32[]{:S(2)}, u32[]{:S(2)}) collective-permute-start(bf16[1,25,4,128]{3,2,1,0:T(4,128)(2,1)S(1)} %get-tuple-element.30), channel_id=1, source_target_pairs={{0,15},{1,0},{2,1},{3,2},{4,3},{5,4},{6,5},{7,6},{8,7},{9,8},{10,9... | collective-permute-start | bytes 76808 | tf_op jit(solution)/shard_map/ppermute | solution.py:20
  37.4 0.9 %collective-permute-done.3 = bf16[1,25,4,128]{3,2,1,0:T(4,128)(2,1)S(1)} collective-permute-done((bf16[1,25,4,128]{3,2,1,0:T(4,128)(2,1)S(1)}, bf16[1,25,4,128]{3,2,1,0:T(4,128)(2,1)S(1)}, u32[]{:S(2)}, u32[]{:S(2)}) %collective-permute-start.3) | collective-permute-done | bytes 25632 | tf_op jit(solution)/shard_map/ppermute | solution.py:20
  38.3 0.1 broadcast.361.clone.1
  38.5 0.4 collective-permute-done.4
  38.9 3.2 %collective-permute-done.5 = bf16[1,25,4,128]{3,2,1,0:T(4,128)(2,1)S(1)} collective-permute-done((bf16[1,25,4,128]{3,2,1,0:T(4,128)(2,1)S(1)}, bf16[1,25,4,128]{3,2,1,0:T(4,128)(2,1)S(1)}, u32[]{:S(2)}, u32[]{:S(2)}) %collective-permute-start.5) | collective-permute-done | bytes 25632 | tf_op jit(solution)/shard_map/ppermute | solution.py:20
  42.1 2.6 %pad_maximum_fusion.1 = bf16[451,4,128]{2,1,0:T(4,128)(2,1)S(1)} fusion(bf16[400,4,128]{2,1,0:T(4,128)(2,1)S(1)} %bitcast.226, bf16[50,4,128]{2,1,0:T(4,128)(2,1)S(1)} %copy.106, bf16[451]{0:T(512)(128)(2,1)S(1)} %pad.40.clone), kind=kLoop, calls=%fused_computation.22 | loop fusion | flops 461824 | bytes 923526 | tf_op jit(solution)/shard_map/concatenate | solution.py:102
  44.8 0.0 slice-start.2
  44.8 2.2 %gather_fusion.3 = bf16[300,4,128]{2,1,0:T(4,128)(2,1)S(1)} fusion(bf16[451,4,128]{2,1,0:T(4,128)(2,1)S(1)} %pad_maximum_fusion.1, s32[1024]{0:T(1024)S(1)} %pad_clamp_fusion.1), kind=kCustom, calls=%fused_computation.3 | custom fusion | bytes 615600 | tf_op jit(solution)/shard_map/gather | solution.py:105
  47.0 5.5 %convolution_bitcast_fusion.2 = f32[50,4,128]{2,1,0:T(4,128)S(1)} fusion(bf16[50,6,4,128]{3,2,1,0:T(4,128)(2,1)S(1)} %bitcast.221, bf16[50,6,128,128]{3,2,1,0:T(8,128)(2,1)} %param.12), kind=kOutput, calls=%fused_computation.16 | convolution fusion | flops 39321600 | bytes 10240000 | tf_op jit(solution)/shard_map/lkcj,lkji->lci/dot_general | solution.py:103
  52.6 1.0 %convolution_bitcast_fusion.1 = f32[50,4,128]{2,1,0:T(4,128)S(1)} fusion(bf16[50,3,128,128]{3,2,1,0:T(8,128)(2,1)S(1)} %bitcast.218, bf16[50,3,4,128]{3,0,2,1:T(8,128)(2,1)S(1)} %pad_maximum_fusion.3), kind=kOutput, calls=%fused_computation.15 | convolution fusion | flops 19660800 | bytes 5171200 | tf_op jit(solution)/shard_map/lkcj,lkji->lci/dot_general | solution.py:112
  53.6 0.1 fusion.71
  53.7 0.1 fusion.72
  53.9 0.1 fusion.79
  54.1 2.1 %gather_fusion.4 = bf16[400,4,128]{2,1,0:T(4,128)(2,1)S(1)} fusion(bf16[51,4,128]{2,1,0:T(4,128)(2,1)S(1)} %concatenate.63.clone, s32[1024]{0:T(1024)S(1)} %pad_clamp_fusion.2), kind=kCustom, calls=%fused_computation.4 | custom fusion | bytes 820800 | tf_op jit(solution)/shard_map/gather | solution.py:101
  56.2 0.1 collective-permute-start.6
  56.3 1.6 %gather_fusion.6 = f32[192]{0:T(256)S(1)} fusion(f32[129]{0:T(256)S(1)} %pad_maximum_fusion.5, s32[1024]{0:T(1024)S(1)} %pad_clamp_fusion), kind=kCustom, calls=%fused_computation.6 | custom fusion | bytes 2304 | tf_op jit(solution)/shard_map/gather | solution.py:116
  57.9 0.7 all_to_all.6
  58.6 5.8 %all-to-all-start = ((f32[16,1,12]{2,1,0:T(1,128)}), f32[16,1,12]{2,1,0:T(1,128)S(1)}, u32[]{:S(2)}, u32[]{:S(2)}) async-start(f32[16,1,12]{2,1,0:T(1,128)} %bitcast.46), calls=%async_computation | async-start | bytes 16384 | tf_op jit(solution)/shard_map/all_to_all | solution.py:117
  64.4 0.1 fusion.43
  64.6 4.4 %collective-permute-start.7 = (bf16[1,25,4,128]{3,2,1,0:T(4,128)(2,1)S(1)}, bf16[1,25,4,128]{3,2,1,0:T(4,128)(2,1)S(1)}, u32[]{:S(2)}, u32[]{:S(2)}) collective-permute-start(bf16[1,25,4,128]{3,2,1,0:T(4,128)(2,1)S(1)} %get-tuple-element.27), channel_id=1, source_target_pairs={{0,15},{1,0},{2,1},{3,2},{4,3},{5,4},{6,5},{7,6},{8,7},{9,8},{10,9... | collective-permute-start | bytes 76808 | tf_op jit(solution)/shard_map/ppermute | solution.py:20
  69.0 1.8 %all-to-all-done = f32[16,1,12]{2,1,0:T(1,128)S(1)} async-done(((f32[16,1,12]{2,1,0:T(1,128)}), f32[16,1,12]{2,1,0:T(1,128)S(1)}, u32[]{:S(2)}, u32[]{:S(2)}) %all-to-all-start) | async-done | bytes 800 | tf_op jit(solution)/shard_map/all_to_all | solution.py:117
  70.8 0.5 broadcast.510
  71.3 0.7 reduce.3
  72.0 0.7 reshape.328
  72.6 0.1 broadcast.361
  72.8 0.9 %collective-permute-done.8 = bf16[1,25,4,128]{3,2,1,0:T(4,128)(2,1)S(1)} collective-permute-done((bf16[1,25,4,128]{3,2,1,0:T(4,128)(2,1)S(1)}, bf16[1,25,4,128]{3,2,1,0:T(4,128)(2,1)S(1)}, u32[]{:S(2)}, u32[]{:S(2)}) %collective-permute-start.8) | collective-permute-done | bytes 25632 | tf_op jit(solution)/shard_map/ppermute | solution.py:20
  73.8 0.0 slice-start.4
  73.8 2.6 %pad_maximum_fusion.2 = bf16[451,4,128]{2,1,0:T(4,128)(2,1)S(1)} fusion(bf16[400,4,128]{2,1,0:T(4,128)(2,1)S(1)} %bitcast.224, bf16[50,4,128]{2,1,0:T(4,128)(2,1)S(1)} %copy.116, bf16[451]{0:T(512)(128)(2,1)S(1)} %pad.40.clone), kind=kLoop, calls=%fused_computation.23 | loop fusion | flops 461824 | bytes 923526 | tf_op jit(solution)/shard_map/concatenate | solution.py:102
  76.4 2.2 %gather_fusion.5 = bf16[300,4,128]{2,1,0:T(4,128)(2,1)S(1)} fusion(bf16[451,4,128]{2,1,0:T(4,128)(2,1)S(1)} %pad_maximum_fusion.2, s32[1024]{0:T(1024)S(1)} %pad_clamp_fusion.1), kind=kCustom, calls=%fused_computation.5 | custom fusion | bytes 615600 | tf_op jit(solution)/shard_map/gather | solution.py:105
  78.7 5.5 %fusion.13 = bf16[50,4,128]{2,1,0:T(4,128)(2,1)S(1)} fusion(bf16[50,6,4,128]{3,2,1,0:T(4,128)(2,1)S(1)} %bitcast.223, bf16[50,6,128,128]{3,2,1,0:T(8,128)(2,1)} %param.12, f32[50,1,128]{2,1,0:T(1,128)S(1)} %get-tuple-element.16, f32[50,1,128]{2,1,0:T(1,128)S(1)} %copy.130, f32[50,1,128]{2,1,0:T(1,128)S(1)} %get-tuple-element.12, f32[50,1,128]{2,1,0:T(1,128)S(1)} %copy.129), kind=kOutput, calls=%fused_computation.20 | convolution fusion | flops 39475200 | bytes 10291200 | tf_op jit(solution)/shard_map/lkcj,lkji->lci/dot_general | solution.py:103
  84.2 1.0 %fusion.7 = f32[50,4,128]{2,1,0:T(4,128)S(1)} fusion(bf16[50,3,128,128]{3,2,1,0:T(8,128)(2,1)S(1)} %bitcast.220, bf16[50,1,4,128]{3,2,0,1:T(4,128)(2,1)S(1)} %get-tuple-element.56, bf16[50,1,4,128]{3,2,0,1:T(4,128)(2,1)S(1)} %bitcast.233, bf16[50,1,4,128]{3,2,0,1:T(4,128)(2,1)S(1)} %get-tuple-element.55), kind=kOutput, calls=%fused_computation.12 | convolution fusion | flops 20121600 | bytes 5171200 | tf_op jit(solution)/shard_map/lkcj,lkji->lci/dot_general | solution.py:112
  85.2 0.6 copy.134
  85.9 0.6 copy.135
  (71 shorter events, 1.0 us)
Async XLA Ops:
  5.4 13.1 %collective-permute-start = (bf16[1,25,4,128]{3,2,1,0:T(4,128)(2,1)S(1)}, bf16[1,25,4,128]{3,2,1,0:T(4,128)(2,1)S(1)}, u32[]{:S(2)}, u32[]{:S(2)}) collective-permute-start(bf16[1,25,4,128]{3,2,1,0:T(4,128)(2,1)S(1)} %get-tuple-element.34), channel_id=1, source_target_pairs={{0,1},{1,2},{2,3},{3,4},{4,5},{5,6},{6,7},{7,8},{8,9},{9,10},{10,1... | collective-permute-start | bytes 76808 | tf_op jit(solution)/shard_map/ppermute | solution.py:20
  5.9 12.7 %collective-permute-start.1 = (bf16[1,25,4,128]{3,2,1,0:T(4,128)(2,1)S(1)}, bf16[1,25,4,128]{3,2,1,0:T(4,128)(2,1)S(1)}, u32[]{:S(2)}, u32[]{:S(2)}) collective-permute-start(bf16[1,25,4,128]{3,2,1,0:T(4,128)(2,1)S(1)} %get-tuple-element.33), channel_id=1, source_target_pairs={{0,15},{1,0},{2,1},{3,2},{4,3},{5,4},{6,5},{7,6},{8,7},{9,8},{10,9... | collective-permute-start | bytes 76808 | tf_op jit(solution)/shard_map/ppermute | solution.py:20
  10.9 7.7 %collective-permute-start.2 = (bf16[1,25,4,128]{3,2,1,0:T(4,128)(2,1)S(1)}, bf16[1,25,4,128]{3,2,1,0:T(4,128)(2,1)S(1)}, u32[]{:S(2)}, u32[]{:S(2)}) collective-permute-start(bf16[1,25,4,128]{3,2,1,0:T(4,128)(2,1)S(1)} %get-tuple-element.32), channel_id=1, source_target_pairs={{0,8},{1,9},{2,10},{3,11},{4,12},{5,13},{6,14},{7,15},{8,0},{9,1},... | collective-permute-start | bytes 76808 | tf_op jit(solution)/shard_map/ppermute | solution.py:20
  21.3 7.7 %slice-start = ((s8[4915200]{0:T(1024)(128)(4,1)}), s8[720896]{0:T(1024)(128)(4,1)S(1)}, s32[]{:S(2)}) async-start(s8[4915200]{0:T(1024)(128)(4,1)} %bitcast.215), calls=%async_computation.1 | async-start | bytes 1441792
  23.5 5.5 %slice-start.1 = ((s8[4915200]{0:T(1024)(128)(4,1)}), s8[4194304]{0:T(1024)(128)(4,1)S(1)}, s32[]{:S(2)}) async-start(s8[4915200]{0:T(1024)(128)(4,1)} %bitcast.215), calls=%async_computation.2 | async-start | bytes 8388608
  29.0 3.4 %copy-start = (f32[128]{0:T(128)S(1)}, f32[128]{0:T(128)}, u32[]{:S(2)}) copy-start(f32[128]{0:T(128)} %param.17) | copy-start | bytes 1540
  32.3 6.0 %collective-permute-start.3 = (bf16[1,25,4,128]{3,2,1,0:T(4,128)(2,1)S(1)}, bf16[1,25,4,128]{3,2,1,0:T(4,128)(2,1)S(1)}, u32[]{:S(2)}, u32[]{:S(2)}) collective-permute-start(bf16[1,25,4,128]{3,2,1,0:T(4,128)(2,1)S(1)} %get-tuple-element.31), channel_id=1, source_target_pairs={{0,1},{1,2},{2,3},{3,4},{4,5},{5,6},{6,7},{7,8},{8,9},{9,10},{10,1... | collective-permute-start | bytes 76808 | tf_op jit(solution)/shard_map/ppermute | solution.py:20
  32.7 6.2 %collective-permute-start.4 = (bf16[1,25,4,128]{3,2,1,0:T(4,128)(2,1)S(1)}, bf16[1,25,4,128]{3,2,1,0:T(4,128)(2,1)S(1)}, u32[]{:S(2)}, u32[]{:S(2)}) collective-permute-start(bf16[1,25,4,128]{3,2,1,0:T(4,128)(2,1)S(1)} %get-tuple-element.30), channel_id=1, source_target_pairs={{0,15},{1,0},{2,1},{3,2},{4,3},{5,4},{6,5},{7,6},{8,7},{9,8},{10,9... | collective-permute-start | bytes 76808 | tf_op jit(solution)/shard_map/ppermute | solution.py:20
  37.4 4.7 %collective-permute-start.5 = (bf16[1,25,4,128]{3,2,1,0:T(4,128)(2,1)S(1)}, bf16[1,25,4,128]{3,2,1,0:T(4,128)(2,1)S(1)}, u32[]{:S(2)}, u32[]{:S(2)}) collective-permute-start(bf16[1,25,4,128]{3,2,1,0:T(4,128)(2,1)S(1)} %get-tuple-element.29), channel_id=1, source_target_pairs={{0,8},{1,9},{2,10},{3,11},{4,12},{5,13},{6,14},{7,15},{8,0},{9,1},... | collective-permute-start | bytes 76808 | tf_op jit(solution)/shard_map/ppermute | solution.py:20
  44.8 7.8 %slice-start.2 = ((s8[4915200]{0:T(1024)(128)(4,1)}), s8[720896]{0:T(1024)(128)(4,1)S(1)}, s32[]{:S(2)}) async-start(s8[4915200]{0:T(1024)(128)(4,1)} %bitcast.217), calls=%async_computation.3 | async-start | bytes 1441792
  47.0 5.6 %slice-start.3 = ((s8[4915200]{0:T(1024)(128)(4,1)}), s8[4194304]{0:T(1024)(128)(4,1)S(1)}, s32[]{:S(2)}) async-start(s8[4915200]{0:T(1024)(128)(4,1)} %bitcast.217), calls=%async_computation.4 | async-start | bytes 8388608
  56.2 16.4 %collective-permute-start.6 = (bf16[1,25,4,128]{3,2,1,0:T(4,128)(2,1)S(1)}, bf16[1,25,4,128]{3,2,1,0:T(4,128)(2,1)S(1)}, u32[]{:S(2)}, u32[]{:S(2)}) collective-permute-start(bf16[1,25,4,128]{3,2,1,0:T(4,128)(2,1)S(1)} %get-tuple-element.28), channel_id=1, source_target_pairs={{0,1},{1,2},{2,3},{3,4},{4,5},{5,6},{6,7},{7,8},{8,9},{9,10},{10,1... | collective-permute-start | bytes 76808 | tf_op jit(solution)/shard_map/ppermute | solution.py:20
  58.6 12.2 %all-to-all-start = ((f32[16,1,12]{2,1,0:T(1,128)}), f32[16,1,12]{2,1,0:T(1,128)S(1)}, u32[]{:S(2)}, u32[]{:S(2)}) async-start(f32[16,1,12]{2,1,0:T(1,128)} %bitcast.46), calls=%async_computation | async-start | bytes 16384 | tf_op jit(solution)/shard_map/all_to_all | solution.py:117
  64.6 8.2 %collective-permute-start.7 = (bf16[1,25,4,128]{3,2,1,0:T(4,128)(2,1)S(1)}, bf16[1,25,4,128]{3,2,1,0:T(4,128)(2,1)S(1)}, u32[]{:S(2)}, u32[]{:S(2)}) collective-permute-start(bf16[1,25,4,128]{3,2,1,0:T(4,128)(2,1)S(1)} %get-tuple-element.27), channel_id=1, source_target_pairs={{0,15},{1,0},{2,1},{3,2},{4,3},{5,4},{6,5},{7,6},{8,7},{9,8},{10,9... | collective-permute-start | bytes 76808 | tf_op jit(solution)/shard_map/ppermute | solution.py:20
  69.0 4.7 %collective-permute-start.8 = (bf16[1,25,4,128]{3,2,1,0:T(4,128)(2,1)S(1)}, bf16[1,25,4,128]{3,2,1,0:T(4,128)(2,1)S(1)}, u32[]{:S(2)}, u32[]{:S(2)}) collective-permute-start(bf16[1,25,4,128]{3,2,1,0:T(4,128)(2,1)S(1)} %get-tuple-element.26), channel_id=1, source_target_pairs={{0,8},{1,9},{2,10},{3,11},{4,12},{5,13},{6,14},{7,15},{8,0},{9,1},... | collective-permute-start | bytes 76808 | tf_op jit(solution)/shard_map/ppermute | solution.py:20
  73.8 10.4 %slice-start.4 = ((s8[4915200]{0:T(1024)(128)(4,1)}), s8[720896]{0:T(1024)(128)(4,1)S(1)}, s32[]{:S(2)}) async-start(s8[4915200]{0:T(1024)(128)(4,1)} %bitcast.219), calls=%async_computation.5 | async-start | bytes 1441792
  78.6 5.6 %slice-start.5 = ((s8[4915200]{0:T(1024)(128)(4,1)}), s8[4194304]{0:T(1024)(128)(4,1)S(1)}, s32[]{:S(2)}) async-start(s8[4915200]{0:T(1024)(128)(4,1)} %bitcast.219), calls=%async_computation.6 | async-start | bytes 8388608
where the time goes:
time: 87 us; the launch traced here: 86.5 us
  starting transfers between devices  21.7 us (25%)
  local copies, waits for them, and re-layouts  20.8 us (24%)
  matrix products  19.2 us (22%)
  other arithmetic  16.1 us (19%)
  waiting for transfers between devices  7.3 us (8%)
  between operations  1.35 us (2%)
    dot_general x3, matrix products, on_device(): jnp.einsum('lkcj,lkji->lci', tile_pool[explicit_columns], explicit_tiles,...  16.4 us
    ppermute x9, starting transfers between devices, shifted(): return lax.ppermute(value, axis, pairs)  15.9 us
    concatenate x3, other arithmetic, on_device(): jnp.concatenate([rounded, ghosts.reshape(-1, channels, column_count)], 0)  7.91 us
    gather x3, local copies, waits for them, and re-layouts, on_device(): tile_pool[explicit_columns]  6.62 us
    gather x3, local copies, waits for them, and re-layouts, on_device(): ghosts = fetch_ghosts(rounded[ghost_levels])  6.33 us
    all_to_all x1, starting transfers between devices, on_device(): lax.all_to_all(slot_values, 'tile', split_axis=0, concat_axis=0, tiled=True)  5.8 us
    ppermute x9, waiting for transfers between devices, shifted(): return lax.ppermute(value, axis, pairs)  5.52 us
    unnamed x18, local copies, waits for them, and re-layouts  2.97 us
  transfers between devices with their start and end apart: 10, of which 5 were waited for; matrix products, arithmetic and copies ran while one was open for 12% of the time, Pallas kernels for 0%

commit v1 on v0

v1 whole, which is shorter than its diff:
```python
import jax
import jax.numpy as jnp
from jax import lax
from jax.experimental import pallas as pl
from jax.experimental.pallas import tpu as pltpu
from jax.sharding import PartitionSpec as P

EUPHOTIC = 6
STEPS = 3

max_uptake = 1.0
half_saturation = 0.5
dop_fraction = 0.67
dop_decay = 0.2
time_step = 0.5

MESH = pl.DeviceIdType.MESH
ROWS = 8


def divisor(count, most):
    return max(n for n in range(1, most + 1) if count % n == 0)


def kernel(
    state_ref,
    direction_ref,
    columns_ref,
    wet_ref,
    light_ref,
    martin_ref,
    slots_ref,
    explicit_hbm,
    implicit_hbm,
    state_out,
    tangent_out,
    flux_out,
    local_tiles,
    ghost_tiles,
    implicit_tiles,
    fields,
    middle,
    remineral,
    ghost_mask,
    sending,
    arriving,
    flux_sending,
    flux_arriving,
    local_sem,
    ghost_tile_sem,
    implicit_sem,
    send_sem,
    recv_sem,
    flux_send_sem,
    flux_recv_sem,
):
    tile_count = lax.axis_size("tile")
    me = lax.axis_index("tile")
    tracers, levels, width = state_ref.shape
    slot_count = slots_ref.shape[1]
    chunk = divisor(levels, 10)
    chunks = levels // chunk
    quads = sending.shape[1] // 16
    depth = 3 * width

    def peer_at(offset):
        return lax.rem(me + offset + tile_count, tile_count)

    local_copies = [
        pltpu.make_async_copy(
            explicit_hbm.at[pl.ds(c * chunk, chunk), pl.ds(0, depth), :],
            local_tiles.at[pl.ds(c * chunk, chunk)],
            local_sem.at[c],
        )
        for c in range(chunks)
    ]
    ghost_copy = pltpu.make_async_copy(
        explicit_hbm.at[pl.ds(0, 4 * quads), pl.ds(depth, depth), :],
        ghost_tiles,
        ghost_tile_sem,
    )
    implicit_copies = [
        pltpu.make_async_copy(
            implicit_hbm.at[pl.ds(c * chunk, chunk)],
            implicit_tiles.at[pl.ds(c * chunk, chunk)],
            implicit_sem.at[c],
        )
        for c in range(chunks)
    ]
    for copy in local_copies + [ghost_copy] + implicit_copies:
        copy.start()

    barrier = pltpu.get_barrier_semaphore()
    for offset in range(1, tile_count):
        pl.semaphore_signal(
            barrier, inc=1, device_id={"tile": peer_at(offset)}, device_id_type=MESH
        )

    row = lax.broadcasted_iota(jnp.int32, (ROWS, width), 0)
    upper = row < 4
    depth_count = wet_ref[...].astype(jnp.float32)
    wet_limit = jnp.where(upper, jnp.broadcast_to(depth_count, (ROWS, width)), 0.0)
    light = light_ref[...]
    martin = martin_ref[...]

    zeros = jnp.zeros((ROWS, width), jnp.float32)
    fields[...] = jnp.zeros_like(fields)
    middle[pl.ds(0, ROWS), :] = zeros
    middle[pl.ds((levels + 1) * ROWS, ROWS), :] = zeros
    for c in range(tracers):
        fields[pl.ds(ROWS + c, levels, stride=ROWS), :] = state_ref[c]
        fields[pl.ds(ROWS + tracers + c, levels, stride=ROWS), :] = direction_ref[c]

    level = lax.broadcasted_iota(jnp.int32, (levels, width), 0).astype(jnp.float32)

    def passing(at):
        ratio = jnp.log(jnp.maximum(at + 1.0, 1.0) / EUPHOTIC)
        reaching = jnp.where(at >= EUPHOTIC - 1, jnp.exp(-1.5 * martin * ratio), 1.0)
        kept = jnp.where(at < depth_count - 1.0, reaching, 0.0)
        return jnp.where(at < 0.0, 1.0, kept)

    remineral[...] = time_step * (passing(level - 1.0) - passing(level))

    for k in range(3):
        for l in range(4 * quads):
            shared = (columns_ref[l : l + 1, 3 + k : 4 + k] != levels).astype(jnp.float32)
            ghost_mask[k, pl.ds(4 * l, 4), :] = jnp.broadcast_to(shared, (4, width))
    flux_sending[...] = jnp.zeros_like(flux_sending)

    even = jnp.where((row == 0) | (row == 2), time_step * dop_decay, 0.0)
    odd = jnp.where((row == 1) | (row == 3), time_step * dop_decay, 0.0)
    lit = lax.broadcasted_iota(jnp.int32, (ROWS, width), 0).astype(jnp.float32)
    strength = jnp.where(
        (lit < EUPHOTIC) & (lit < depth_count),
        max_uptake * light * jnp.exp(-2.0 * lit / EUPHOTIC),
        0.0,
    )
    uptake_share = time_step * jnp.where(
        even > 0.0, -1.0, jnp.where(odd > 0.0, dop_fraction, 0.0)
    )

    def at_level(l):
        return pl.ds(pl.multiple_of((l + 1) * ROWS, ROWS), ROWS)

    total = jnp.zeros((1, width), jnp.float32)
    flux_copies = []
    for step in range(STEPS):
        for q in range(quads):
            parts = [fields[at_level(4 * q + j), :] for j in range(4)]
            pairs = [
                jnp.where(upper, parts[2 * h], pltpu.roll(parts[2 * h + 1], 4, 0))
                for h in range(2)
            ]
            sending[step, pl.ds(16 * q, 16), :] = jnp.concatenate(pairs, 0).astype(
                jnp.bfloat16
            )
        if step == 0:
            pl.semaphore_wait(barrier, tile_count - 1)
        copies = []
        for k, offset in enumerate((1, -1, tile_count // 2)):
            copies.append(
                pltpu.make_async_remote_copy(
                    src_ref=sending.at[step],
                    dst_ref=arriving.at[step, k],
                    send_sem=send_sem.at[step, k],
                    recv_sem=recv_sem.at[step, k],
                    device_id={"tile": peer_at(offset)},
                    device_id_type=MESH,
                )
            )
        for copy in copies:
            copy.start()

        phosphate = fields[pl.ds(ROWS, ROWS, stride=ROWS), :]
        direction = fields[pl.ds(ROWS + tracers, ROWS, stride=ROWS), :]
        inverse = 1.0 / (half_saturation**2 + phosphate * phosphate)
        uptake = strength * (phosphate * phosphate) * inverse
        uptake_slope = (
            strength
            * (2.0 * half_saturation**2 * phosphate * inverse)
            * (direction * inverse)
        )
        export = (1.0 - dop_fraction) * jnp.sum(uptake, 0, keepdims=True)
        export_slope = (1.0 - dop_fraction) * jnp.sum(uptake_slope, 0, keepdims=True)
        total = total + export
        sinking = jnp.where(row == 0, export, jnp.where(row == 2, export_slope, 0.0))

        if step == STEPS - 1:
            by_column = jnp.transpose(jnp.broadcast_to(total, (width, width)))
            by_column = by_column[:, :slot_count]
            column = lax.broadcasted_iota(jnp.int32, (width, slot_count), 0)

            def fill(b, carry):
                picked = jnp.where(column == slots_ref[pl.ds(b, 1), :], by_column, 0.0)
                flux_sending[b, 0:1, 0:slot_count] = jnp.sum(picked, 0, keepdims=True)
                return carry

            lax.fori_loop(0, tile_count, fill, 0, unroll=2)
            for offset in range(1, tile_count):
                flux_copies.append(
                    pltpu.make_async_remote_copy(
                        src_ref=flux_sending.at[peer_at(offset)],
                        dst_ref=flux_arriving.at[me],
                        send_sem=flux_send_sem.at[offset],
                        recv_sem=flux_recv_sem.at[offset],
                        device_id={"tile": peer_at(offset)},
                        device_id_type=MESH,
                    )
                )
            for copy in flux_copies:
                copy.start()

        def explicit_chunk(c, carry):
            for i in range(chunk):
                l = c * chunk + i
                here = fields[at_level(l), :]
                above = fields[at_level(l - 1), :]
                below = fields[at_level(l + 1), :]
                source = jnp.concatenate([here, above, below], 1).astype(jnp.bfloat16)
                carried = jnp.dot(
                    source, local_tiles[l], preferred_element_type=jnp.float32
                )
                decay = even * pltpu.roll(here, ROWS - 1, 0) - odd * here
                decay = jnp.where(l.astype(jnp.float32) < wet_limit, decay, 0.0)
                middle[at_level(l), :] = (
                    carried + decay + remineral[pl.ds(l, 1), :] * sinking
                )
            return carry

        def implicit_chunk(c, carry):
            for i in range(chunk):
                l = c * chunk + i
                source = jnp.concatenate(
                    [middle[at_level(l + k - 1), :] for k in range(3)], 1
                ).astype(jnp.bfloat16)
                settled = jnp.dot(
                    source, implicit_tiles[l], preferred_element_type=jnp.float32
                )
                fields[at_level(l), :] = jnp.where(
                    l.astype(jnp.float32) < wet_limit, settled, 0.0
                )
            return carry

        if step == 0:
            for c in range(chunks):
                local_copies[c].wait()
                lax.fori_loop(c, c + 1, explicit_chunk, 0)
        else:
            lax.fori_loop(0, chunks, explicit_chunk, 0)

        for l in range(EUPHOTIC):
            share = jnp.where(
                row < 2, uptake[l : l + 1, :], uptake_slope[l : l + 1, :]
            )
            middle[at_level(l), :] = middle[at_level(l), :] + uptake_share * share

        if step == 0:
            ghost_copy.wait()
        for copy in copies:
            copy.wait_recv()

        def ghost_quad(q, carry):
            rows = pl.ds(pl.multiple_of(16 * q, 16), 16)
            source = jnp.concatenate(
                [
                    arriving[step, k, rows, :].astype(jnp.float32) * ghost_mask[k, rows, :]
                    for k in range(3)
                ],
                1,
            ).astype(jnp.bfloat16)
            for j in range(4):
                l = 4 * q + j
                carried = jnp.dot(
                    source, ghost_tiles[l], preferred_element_type=jnp.float32
                )[8 * (j // 2) : 8 * (j // 2) + 8]
                if j % 2:
                    carried = pltpu.roll(carried, 4, 0)
                middle[at_level(l), :] = middle[at_level(l), :] + jnp.where(
                    upper, carried, 0.0
                )
            return carry

        lax.fori_loop(0, quads, ghost_quad, 0)

        if step == 0:
            for c in range(chunks):
                implicit_copies[c].wait()
                lax.fori_loop(c, c + 1, implicit_chunk, 0)
        else:
            lax.fori_loop(0, chunks, implicit_chunk, 0)
        for copy in copies:
            copy.wait_send()

    for c in range(tracers):
        state_out[c] = fields[pl.ds(ROWS + c, levels, stride=ROWS), :]
        tangent_out[c] = fields[pl.ds(ROWS + tracers + c, levels, stride=ROWS), :]
    for copy in flux_copies:
        copy.wait()
    flux_arriving[me] = flux_sending[me]
    for s in range(tile_count):
        flux_out[s : s + 1, :] = flux_arriving[s, 0:1, 0:slot_count]


def on_device(
    tracer_state,
    krylov_direction,
    explicit_tiles,
    implicit_tiles,
    explicit_columns,
    ghost_levels,
    wet_levels,
    surface_light,
    martin_exponent,
    column_slots,
):
    levels, width = tracer_state.shape[1:]
    tile_count = lax.axis_size("tile")
    slot_count = column_slots.shape[1]
    quads = -(-ghost_levels.shape[1] // 4)
    chunks = levels // divisor(levels, 10)
    vmem = pl.BlockSpec(memory_space=pltpu.VMEM)
    anywhere = pl.BlockSpec(memory_space=pl.ANY)
    state, tangent, flux = pl.pallas_call(
        kernel,
        out_shape=(
            jax.ShapeDtypeStruct(tracer_state.shape, jnp.float32),
            jax.ShapeDtypeStruct(krylov_direction.shape, jnp.float32),
            jax.ShapeDtypeStruct((tile_count, slot_count), jnp.float32),
        ),
        in_specs=[vmem] * 7 + [anywhere] * 2,
        out_specs=(vmem, vmem, vmem),
        scratch_shapes=[
            pltpu.VMEM((levels, 3 * width, width), jnp.bfloat16),
            pltpu.VMEM((4 * quads, 3 * width, width), jnp.bfloat16),
            pltpu.VMEM((levels, 3 * width, width), jnp.bfloat16),
            pltpu.VMEM(((levels + 2) * ROWS, width), jnp.float32),
            pltpu.VMEM(((levels + 2) * ROWS, width), jnp.float32),
            pltpu.VMEM((levels, width), jnp.float32),
            pltpu.VMEM((3, 16 * quads, width), jnp.float32),
            pltpu.VMEM((STEPS, 16 * quads, width), jnp.bfloat16),
            pltpu.VMEM((STEPS, 3, 16 * quads, width), jnp.bfloat16),
            pltpu.VMEM((tile_count, ROWS, width), jnp.float32),
            pltpu.VMEM((tile_count, ROWS, width), jnp.float32),
            pltpu.SemaphoreType.DMA((chunks,)),
            pltpu.SemaphoreType.DMA,
            pltpu.SemaphoreType.DMA((chunks,)),
            pltpu.SemaphoreType.DMA((STEPS, 3)),
            pltpu.SemaphoreType.DMA((STEPS, 3)),
            pltpu.SemaphoreType.DMA((tile_count,)),
            pltpu.SemaphoreType.DMA((tile_count,)),
        ],
        compiler_params=pltpu.CompilerParams(
            collective_id=0, has_side_effects=True, vmem_limit_bytes=40 << 20
        ),
    )(
        tracer_state,
        krylov_direction,
        explicit_columns,
        wet_levels.reshape(1, width),
        surface_light.reshape(1, width),
        martin_exponent.reshape(1, width),
        column_slots,
        explicit_tiles.reshape(levels, -1, width),
        implicit_tiles.reshape(levels, -1, width),
    )
    return (state, tangent, flux.reshape(-1))


def solution(mesh):
    return jax.shard_map(
        on_device,
        mesh=mesh,
        in_specs=(
            P(None, None, ("groups", "tile")),
            P(None, None, ("groups", "tile")),
            P("tile", None, None, None),
            P("tile", None, None, None),
            P("tile", None),
            P("tile", None),
            P("tile"),
            P(("groups", "tile")),
            P(("groups", "tile")),
            P("tile", None),
        ),
        out_specs=(
            P(None, None, ("groups", "tile")),
            P(None, None, ("groups", "tile")),
            P(("groups", "tile")),
        ),
        check_vma=False,
    )
```

time: 87 us -> 38 us (0.44)
  Pallas kernels: 0 us -> 27.6 us
  starting transfers between devices: 21.7 us -> 0 us
  matrix products: 19.2 us -> 0 us
  other arithmetic: 16.1 us -> 0 us
  local copies, waits for them, and re-layouts: 20.8 us -> 9.4 us
  waiting for transfers between devices: 7.3 us -> 0 us
    pallas_call x0 -> x1, Pallas kernels: none -> 27.6 us  [on_device(): pl.pallas_call(kernel, out_shape=(jax.ShapeDtypeStruct(tracer_state.shape...]
    dot_general x6 -> x0, matrix products: 19.2 us -> none  [the longest x3 16.4 us: on_device(): jnp.einsum('lkcj,lkji->lci', tile_pool[explicit_columns], explicit_tiles,...]
    ppermute x9 -> x0, starting transfers between devices: 15.9 us -> none  [shifted(): return lax.ppermute(value, axis, pairs)]
    gather x7 -> x0, local copies, waits for them, and re-layouts: 14.6 us -> none  [the longest x3 6.62 us: on_device(): tile_pool[explicit_columns]]
    concatenate x4 -> x0, other arithmetic: 7.92 us -> none  [the longest x3 7.91 us: on_device(): jnp.concatenate([rounded, ghosts.reshape(-1, channels, column_count)], 0)]
    all_to_all x1 -> x0, starting transfers between devices: 5.8 us -> none  [on_device(): lax.all_to_all(slot_values, 'tile', split_axis=0, concat_axis=0, tiled=True)]
    unnamed x18 -> x15, local copies, waits for them, and re-layouts: 2.97 us -> 8.75 us
    ppermute x9 -> x0, waiting for transfers between devices: 5.52 us -> none  [shifted(): return lax.ppermute(value, axis, pairs)]
  transfers between devices with their start and end apart: 10 -> 0, of which waited for: 5 -> 0; matrix products, arithmetic and copies ran while one was open for 12% -> 0% of each run, Pallas kernels for 0% -> 0%
where the time goes in v1:
time: 38 us; the launch traced here: 37.7 us
  Pallas kernels  27.6 us (73%)
  local copies, waits for them, and re-layouts  9.4 us (25%)
  between operations  0.65 us (2%)
    pallas_call x1, Pallas kernels, on_device(): pl.pallas_call(kernel, out_shape=(jax.ShapeDtypeStruct(tracer_state.shape...  27.6 us
    unnamed x15, local copies, waits for them, and re-layouts  8.75 us

profile of v1, /device:TPU:0, one launch (start us, length us, event | category | flops | bytes accessed | tf_op | source)
XLA Modules:
  0.0 37.7 jit_solution(9064412077040914454)
XLA Ops:
  0.6 0.8 %copy.14.columns_ref = s32[50,6]{1,0:T(8,128)S(1)} copy(s32[50,6]{0,1:T(8,128)} %param.14) | data formatting | bytes 2400 | tf_op args[4]
  1.4 0.8 %copy.12.state_ref = f32[2,50,128]{2,1,0:T(8,128)S(1)} copy(f32[2,50,128]{2,0,1:T(2,128)} %param.10) | data formatting | bytes 102400 | tf_op args[0]
  2.2 0.8 %copy.13.direction_ref = f32[2,50,128]{2,1,0:T(8,128)S(1)} copy(f32[2,50,128]{2,0,1:T(2,128)} %param.11) | data formatting | bytes 102400 | tf_op args[1]
  3.0 0.0 copy-start
  3.0 2.4 %copy-done = bf16[50,3,128,128]{3,2,1,0:T(8,128)(2,1)S(1)} copy-done((bf16[50,3,128,128]{3,2,1,0:T(8,128)(2,1)S(1)}, bf16[50,3,128,128]{3,2,1,0:T(8,128)(2,1)}, u32[]{:S(2)}) %copy-start) | copy-done | bytes 4915224
  5.4 0.0 copy-start.1
  5.4 0.7 %copy-done.1 = s32[16,12]{1,0:T(8,128)S(1)} copy-done((s32[16,12]{1,0:T(8,128)S(1)}, s32[16,12]{1,0:T(8,128)}, u32[]{:S(2)}) %copy-start.1) | copy-done | bytes 792
  6.1 0.0 copy-start.2
  6.1 0.7 %copy-done.2 = s32[128]{0:T(128)S(1)} copy-done((s32[128]{0:T(128)S(1)}, s32[128]{0:T(128)}, u32[]{:S(2)}) %copy-start.2) | copy-done | bytes 536
  6.8 0.0 copy-start.3
  6.8 0.7 %copy-done.3 = f32[128]{0:T(128)S(1)} copy-done((f32[128]{0:T(128)S(1)}, f32[128]{0:T(128)}, u32[]{:S(2)}) %copy-start.3) | copy-done | bytes 536
  7.4 0.0 copy-start.4
  7.4 0.7 %copy-done.4 = f32[128]{0:T(128)S(1)} copy-done((f32[128]{0:T(128)S(1)}, f32[128]{0:T(128)}, u32[]{:S(2)}) %copy-start.4) | copy-done | bytes 536
  8.1 27.6 %shard_map.112 = (f32[2,50,128]{2,1,0:T(8,128)S(1)}, f32[2,50,128]{2,1,0:T(8,128)S(1)}, f32[16,12]{1,0:T(8,128)S(1)}) custom-call(f32[2,50,128]{2,1,0:T(8,128)S(1)} %copy.12.state_ref, f32[2,50,128]{2,1,0:T(8,128)S(1)} %copy.13.direction_ref, s32[50,6]{1,0:T(8,128)S(1)} %copy.14.columns_ref, s32[1,128]{1,0:T(1,128)S(1)} %bitcast.6, f32[1,128]{1,0:T(1,128)S(1)} %bitcast.7, ...), custom_call_target="tpu_custom_call" | custom-call | tf_op jit(solution)/shard_map/pallas_call | solution.py:323
  35.7 0.6 %copy.15 = f32[2,50,128]{2,0,1:T(2,128)} copy(f32[2,50,128]{2,1,0:T(8,128)S(1)} %get-tuple-element.9) | data formatting | bytes 102400
  36.4 0.7 %reshape.29 = f32[192]{0:T(256)} reshape(f32[16,12]{1,0:T(8,128)S(1)} %get-tuple-element.8) | data formatting | bytes 1536 | tf_op jit(solution)/shard_map/reshape | solution.py:366
  37.0 0.6 %copy.16 = f32[2,50,128]{2,0,1:T(2,128)} copy(f32[2,50,128]{2,1,0:T(8,128)S(1)} %get-tuple-element.10) | data formatting | bytes 102400
Async XLA Ops:
  3.0 2.4 %copy-start = (bf16[50,3,128,128]{3,2,1,0:T(8,128)(2,1)S(1)}, bf16[50,3,128,128]{3,2,1,0:T(8,128)(2,1)}, u32[]{:S(2)}) copy-start(bf16[50,3,128,128]{3,2,1,0:T(8,128)(2,1)} %param.13) | copy-start | bytes 14745604
  5.4 0.7 %copy-start.1 = (s32[16,12]{1,0:T(8,128)S(1)}, s32[16,12]{1,0:T(8,128)}, u32[]{:S(2)}) copy-start(s32[16,12]{1,0:T(8,128)} %slots_ref.1) | copy-start | bytes 2308
  6.1 0.7 %copy-start.2 = (s32[128]{0:T(128)S(1)}, s32[128]{0:T(128)}, u32[]{:S(2)}) copy-start(s32[128]{0:T(128)} %param.15) | copy-start | bytes 1540
  6.8 0.7 %copy-start.3 = (f32[128]{0:T(128)S(1)}, f32[128]{0:T(128)}, u32[]{:S(2)}) copy-start(f32[128]{0:T(128)} %param.16) | copy-start | bytes 1540
  7.4 0.7 %copy-start.4 = (f32[128]{0:T(128)S(1)}, f32[128]{0:T(128)}, u32[]{:S(2)}) copy-start(f32[128]{0:T(128)} %param.17) | copy-start | bytes 1540

commit v2 on v1

--- a/solution.py
+++ b/solution.py
@@ -23,6 +23,18 @@
 
 
 def kernel(
+    state_hbm,
+    direction_hbm,
+    columns_hbm,
+    wet_hbm,
+    light_hbm,
+    martin_hbm,
+    slots_hbm,
+    explicit_hbm,
+    implicit_hbm,
+    state_out,
+    tangent_out,
+    flux_out,
     state_ref,
     direction_ref,
     columns_ref,
@@ -30,11 +42,7 @@
     light_ref,
     martin_ref,
     slots_ref,
-    explicit_hbm,
-    implicit_hbm,
-    state_out,
-    tangent_out,
-    flux_out,
+    small_sem,
     local_tiles,
     ghost_tiles,
     implicit_tiles,
@@ -56,7 +64,7 @@
 ):
     tile_count = lax.axis_size("tile")
     me = lax.axis_index("tile")
-    tracers, levels, width = state_ref.shape
+    levels, tracers, width = state_hbm.shape
     slot_count = slots_ref.shape[1]
     chunk = divisor(levels, 10)
     chunks = levels // chunk
@@ -87,7 +95,21 @@
         )
         for c in range(chunks)
     ]
-    for copy in local_copies + [ghost_copy] + implicit_copies:
+    small_copies = [
+        pltpu.make_async_copy(source, target, small_sem.at[i])
+        for i, (source, target) in enumerate(
+            (
+                (state_hbm, state_ref),
+                (direction_hbm, direction_ref),
+                (wet_hbm, wet_ref),
+                (light_hbm, light_ref),
+                (martin_hbm, martin_ref),
+                (columns_hbm, columns_ref),
+                (slots_hbm, slots_ref),
+            )
+        )
+    ]
+    for copy in small_copies + local_copies + [ghost_copy] + implicit_copies:
         copy.start()
 
     barrier = pltpu.get_barrier_semaphore()
@@ -95,6 +117,11 @@
         pl.semaphore_signal(
             barrier, inc=1, device_id={"tile": peer_at(offset)}, device_id_type=MESH
         )
+
+    fields[...] = jnp.zeros_like(fields)
+    flux_sending[...] = jnp.zeros_like(flux_sending)
+    for copy in small_copies:
+        copy.wait()
 
     row = lax.broadcasted_iota(jnp.int32, (ROWS, width), 0)
     upper = row < 4
@@ -104,12 +131,11 @@
     martin = martin_ref[...]
 
     zeros = jnp.zeros((ROWS, width), jnp.float32)
-    fields[...] = jnp.zeros_like(fields)
     middle[pl.ds(0, ROWS), :] = zeros
     middle[pl.ds((levels + 1) * ROWS, ROWS), :] = zeros
-    for c in range(tracers):
-        fields[pl.ds(ROWS + c, levels, stride=ROWS), :] = state_ref[c]
-        fields[pl.ds(ROWS + tracers + c, levels, stride=ROWS), :] = direction_ref[c]
+    for l in range(levels):
+        fields[pl.ds((l + 1) * ROWS, tracers), :] = state_ref[l]
+        fields[pl.ds((l + 1) * ROWS + tracers, tracers), :] = direction_ref[l]
 
     level = lax.broadcasted_iota(jnp.int32, (levels, width), 0).astype(jnp.float32)
 
@@ -123,9 +149,8 @@
 
     for k in range(3):
         for l in range(4 * quads):
-            shared = (columns_ref[l : l + 1, 3 + k : 4 + k] != levels).astype(jnp.float32)
+            shared = (columns_ref[3 + k : 4 + k, l : l + 1] != levels).astype(jnp.float32)
             ghost_mask[k, pl.ds(4 * l, 4), :] = jnp.broadcast_to(shared, (4, width))
-    flux_sending[...] = jnp.zeros_like(flux_sending)
 
     even = jnp.where((row == 0) | (row == 2), time_step * dop_decay, 0.0)
     odd = jnp.where((row == 1) | (row == 3), time_step * dop_decay, 0.0)
@@ -291,9 +316,9 @@
         for copy in copies:
             copy.wait_send()
 
-    for c in range(tracers):
-        state_out[c] = fields[pl.ds(ROWS + c, levels, stride=ROWS), :]
-        tangent_out[c] = fields[pl.ds(ROWS + tracers + c, levels, stride=ROWS), :]
+    for l in range(levels):
+        state_out[l] = fields[pl.ds((l + 1) * ROWS, tracers), :]
+        tangent_out[l] = fields[pl.ds((l + 1) * ROWS + tracers, tracers), :]
     for copy in flux_copies:
         copy.wait()
     flux_arriving[me] = flux_sending[me]
@@ -313,7 +338,7 @@
     martin_exponent,
     column_slots,
 ):
-    levels, width = tracer_state.shape[1:]
+    tracers, levels, width = tracer_state.shape
     tile_count = lax.axis_size("tile")
     slot_count = column_slots.shape[1]
     quads = -(-ghost_levels.shape[1] // 4)
@@ -323,13 +348,21 @@
     state, tangent, flux = pl.pallas_call(
         kernel,
         out_shape=(
-            jax.ShapeDtypeStruct(tracer_state.shape, jnp.float32),
-            jax.ShapeDtypeStruct(krylov_direction.shape, jnp.float32),
+            jax.ShapeDtypeStruct((levels, tracers, width), jnp.float32),
+            jax.ShapeDtypeStruct((levels, tracers, width), jnp.float32),
             jax.ShapeDtypeStruct((tile_count, slot_count), jnp.float32),
         ),
-        in_specs=[vmem] * 7 + [anywhere] * 2,
+        in_specs=[anywhere] * 9,
         out_specs=(vmem, vmem, vmem),
         scratch_shapes=[
+            pltpu.VMEM((levels, tracers, width), jnp.float32),
+            pltpu.VMEM((levels, tracers, width), jnp.float32),
+            pltpu.VMEM(explicit_columns.shape[::-1], jnp.int32),
+            pltpu.VMEM((1, width), jnp.int32),
+            pltpu.VMEM((1, width), jnp.float32),
+            pltpu.VMEM((1, width), jnp.float32),
+            pltpu.VMEM(column_slots.shape, jnp.int32),
+            pltpu.SemaphoreType.DMA((7,)),
             pltpu.VMEM((levels, 3 * width, width), jnp.bfloat16),
             pltpu.VMEM((4 * quads, 3 * width, width), jnp.bfloat16),
             pltpu.VMEM((levels, 3 * width, width), jnp.bfloat16),
@@ -350,12 +383,12 @@
             pltpu.SemaphoreType.DMA((tile_count,)),
         ],
         compiler_params=pltpu.CompilerParams(
-            collective_id=0, has_side_effects=True, vmem_limit_bytes=40 << 20
+            collective_id=0, has_side_effects=True, vmem_limit_bytes=60 << 20
         ),
     )(
-        tracer_state,
-        krylov_direction,
-        explicit_columns,
+        tracer_state.transpose(1, 0, 2),
+        krylov_direction.transpose(1, 0, 2),
+        explicit_columns.T,
         wet_levels.reshape(1, width),
         surface_light.reshape(1, width),
         martin_exponent.reshape(1, width),
@@ -363,7 +396,7 @@
         explicit_tiles.reshape(levels, -1, width),
         implicit_tiles.reshape(levels, -1, width),
     )
-    return (state, tangent, flux.reshape(-1))
+    return (state.transpose(1, 0, 2), tangent.transpose(1, 0, 2), flux.reshape(-1))
 
 
 def solution(mesh):

time: 38 us -> 33.3 us (0.88)
  local copies, waits for them, and re-layouts: 9.4 us -> 4.2 us
  Pallas kernels: 27.6 us -> 28.2 us
    unnamed x15 -> x2, local copies, waits for them, and re-layouts: 8.75 us -> 2.85 us
    reshape x1, local copies, waits for them, and re-layouts: 0.65 us -> 1.35 us  [on_device(): flux.reshape(-1)]
    pallas_call x1, Pallas kernels: 27.6 us -> 28.2 us  [on_device(): pl.pallas_call(kernel, out_shape=(jax.ShapeDtypeStruct((levels, tracers,...]
where the time goes in v2:
time: 33.3 us; the launch traced here: 33 us
  Pallas kernels  28.2 us (85%)
  local copies, waits for them, and re-layouts  4.2 us (13%)
  between operations  0.64 us (2%)
    pallas_call x1, Pallas kernels, on_device(): pl.pallas_call(kernel, out_shape=(jax.ShapeDtypeStruct((levels, tracers,...  28.2 us
    unnamed x2, local copies, waits for them, and re-layouts  2.85 us
    reshape x1, local copies, waits for them, and re-layouts, on_device(): flux.reshape(-1)  1.35 us

profile of v2, /device:TPU:0, one launch (start us, length us, event | category | flops | bytes accessed | tf_op | source)
XLA Modules:
  0.0 33.0 jit_solution(11811912973712322277)
XLA Ops:
  0.6 28.2 %shard_map.112 = (f32[50,2,128]{2,1,0:T(2,128)}, f32[50,2,128]{2,1,0:T(2,128)}, f32[16,12]{1,0:T(8,128)}) custom-call(f32[50,2,128]{2,1,0:T(2,128)} %bitcast.12, f32[50,2,128]{2,1,0:T(2,128)} %bitcast.13, s32[6,50]{1,0:T(8,128)} %bitcast.16, s32[1,128]{1,0:T(1,128)} %bitcast.17, f32[1,128]{1,0:T(1,128)} %bitcast.18, f32[1,128]{1,0:T(1,128)} %bitcast.19, ...), custom_call_target="tpu_custom_call" | custom-call | tf_op jit(solution)/shard_map/pallas_call | solution.py:348
  28.8 1.3 %reshape.29 = f32[192]{0:T(256)} reshape(f32[16,12]{1,0:T(8,128)} %get-tuple-element.8) | data formatting | bytes 1536 | tf_op jit(solution)/shard_map/reshape | solution.py:399
  30.2 1.4 %copy.14 = f32[2,50,128]{2,0,1:T(2,128)} copy(f32[2,50,128]{2,0,1:T(2,128)} %bitcast.15) | data formatting | bytes 102400
  31.6 1.4 %copy.15 = f32[2,50,128]{2,0,1:T(2,128)} copy(f32[2,50,128]{2,0,1:T(2,128)} %bitcast.14) | data formatting | bytes 102400

commit v3 on v2

--- a/solution.py
+++ b/solution.py
@@ -122,9 +122,58 @@
     flux_sending[...] = jnp.zeros_like(flux_sending)
     for copy in small_copies:
         copy.wait()
+    for l in range(levels):
+        fields[pl.ds((l + 1) * ROWS, tracers), :] = state_ref[l]
+        fields[pl.ds((l + 1) * ROWS + tracers, tracers), :] = direction_ref[l]
 
     row = lax.broadcasted_iota(jnp.int32, (ROWS, width), 0)
+    quad_row = lax.broadcasted_iota(jnp.int32, (2 * ROWS, width), 0) // 4
     upper = row < 4
+    pieces = ((0, quads // 2), (quads // 2, quads))
+    ghost_copies = [[] for _ in range(STEPS)]
+
+    def at_level(l):
+        return pl.ds(pl.multiple_of((l + 1) * ROWS, ROWS), ROWS)
+
+    def pack_piece(step, piece):
+        for q in range(*pieces[piece]):
+            parts = [fields[at_level(4 * q + j), :] for j in range(4)]
+            pairs = [
+                jnp.where(upper, parts[2 * h], pltpu.roll(parts[2 * h + 1], 4, 0))
+                for h in range(2)
+            ]
+            sending[step, pl.ds(16 * q, 16), :] = jnp.concatenate(pairs, 0).astype(
+                jnp.bfloat16
+            )
+
+    def start_piece(step, piece):
+        first, last = pieces[piece]
+        rows = pl.ds(16 * first, 16 * (last - first))
+        copies = [
+            pltpu.make_async_remote_copy(
+                src_ref=sending.at[step, rows],
+                dst_ref=arriving.at[step, k, rows],
+                send_sem=send_sem.at[step, piece, k],
+                recv_sem=recv_sem.at[step, piece, k],
+                device_id={"tile": peer_at(offset)},
+                device_id_type=MESH,
+            )
+            for k, offset in ((2, tile_count // 2), (0, 1), (1, -1))
+        ]
+        for copy in copies:
+            copy.start()
+        ghost_copies[step].append(copies)
+
+    def send_piece(step, piece):
+        pack_piece(step, piece)
+        start_piece(step, piece)
+
+    for piece in range(2):
+        pack_piece(0, piece)
+    pl.semaphore_wait(barrier, tile_count - 1)
+    for piece in range(2):
+        start_piece(0, piece)
+
     depth_count = wet_ref[...].astype(jnp.float32)
     wet_limit = jnp.where(upper, jnp.broadcast_to(depth_count, (ROWS, width)), 0.0)
     light = light_ref[...]
@@ -133,9 +182,6 @@
     zeros = jnp.zeros((ROWS, width), jnp.float32)
     middle[pl.ds(0, ROWS), :] = zeros
     middle[pl.ds((levels + 1) * ROWS, ROWS), :] = zeros
-    for l in range(levels):
-        fields[pl.ds((l + 1) * ROWS, tracers), :] = state_ref[l]
-        fields[pl.ds((l + 1) * ROWS + tracers, tracers), :] = direction_ref[l]
 
     level = lax.broadcasted_iota(jnp.int32, (levels, width), 0).astype(jnp.float32)
 
@@ -164,38 +210,18 @@
         even > 0.0, -1.0, jnp.where(odd > 0.0, dop_fraction, 0.0)
     )
 
-    def at_level(l):
-        return pl.ds(pl.multiple_of((l + 1) * ROWS, ROWS), ROWS)
+    def pair_product(first, second, tiles, l):
+        blocks = [jnp.concatenate([part, zeros], 0) for part in first]
+        blocks += [jnp.concatenate([zeros, part], 0) for part in second]
+        return jnp.dot(
+            jnp.concatenate(blocks, 1).astype(jnp.bfloat16),
+            tiles[pl.ds(l, 2)].reshape(2 * depth, width),
+            preferred_element_type=jnp.float32,
+        )
 
     total = jnp.zeros((1, width), jnp.float32)
     flux_copies = []
     for step in range(STEPS):
-        for q in range(quads):
-            parts = [fields[at_level(4 * q + j), :] for j in range(4)]
-            pairs = [
-                jnp.where(upper, parts[2 * h], pltpu.roll(parts[2 * h + 1], 4, 0))
-                for h in range(2)
-            ]
-            sending[step, pl.ds(16 * q, 16), :] = jnp.concatenate(pairs, 0).astype(
-                jnp.bfloat16
-            )
-        if step == 0:
-            pl.semaphore_wait(barrier, tile_count - 1)
-        copies = []
-        for k, offset in enumerate((1, -1, tile_count // 2)):
-            copies.append(
-                pltpu.make_async_remote_copy(
-                    src_ref=sending.at[step],
-                    dst_ref=arriving.at[step, k],
-                    send_sem=send_sem.at[step, k],
-                    recv_sem=recv_sem.at[step, k],
-                    device_id={"tile": peer_at(offset)},
-                    device_id_type=MESH,
-                )
-            )
-        for copy in copies:
-            copy.start()
-
         phosphate = fields[pl.ds(ROWS, ROWS, stride=ROWS), :]
         direction = fields[pl.ds(ROWS + tracers, ROWS, stride=ROWS), :]
         inverse = 1.0 / (half_saturation**2 + phosphate * phosphate)
@@ -236,34 +262,20 @@
                 copy.start()
 
         def explicit_chunk(c, carry):
-            for i in range(chunk):
-                l = c * chunk + i
-                here = fields[at_level(l), :]
-                above = fields[at_level(l - 1), :]
-                below = fields[at_level(l + 1), :]
-                source = jnp.concatenate([here, above, below], 1).astype(jnp.bfloat16)
-                carried = jnp.dot(
-                    source, local_tiles[l], preferred_element_type=jnp.float32
-                )
-                decay = even * pltpu.roll(here, ROWS - 1, 0) - odd * here
-                decay = jnp.where(l.astype(jnp.float32) < wet_limit, decay, 0.0)
-                middle[at_level(l), :] = (
-                    carried + decay + remineral[pl.ds(l, 1), :] * sinking
-                )
-            return carry
-
-        def implicit_chunk(c, carry):
-            for i in range(chunk):
-                l = c * chunk + i
-                source = jnp.concatenate(
-                    [middle[at_level(l + k - 1), :] for k in range(3)], 1
-                ).astype(jnp.bfloat16)
-                settled = jnp.dot(
-                    source, implicit_tiles[l], preferred_element_type=jnp.float32
-                )
-                fields[at_level(l), :] = jnp.where(
-                    l.astype(jnp.float32) < wet_limit, settled, 0.0
-                )
+            for i in range(chunk // 2):
+                l = c * chunk + 2 * i
+                near = [fields[at_level(l + n), :] for n in range(-1, 3)]
+                first, second = (near[1], near[0], near[2]), (near[2], near[1], near[3])
+                carried = pair_product(first, second, local_tiles, l)
+                for n in range(2):
+                    here = near[1 + n]
+                    decay = even * pltpu.roll(here, ROWS - 1, 0) - odd * here
+                    wet = (l + n).astype(jnp.float32) < wet_limit
+                    middle[at_level(l + n), :] = (
+                        carried[n * ROWS : (n + 1) * ROWS]
+                        + jnp.where(wet, decay, 0.0)
+                        + remineral[pl.ds(l + n, 1), :] * sinking
+                    )
             return carry
 
         if step == 0:
@@ -279,42 +291,67 @@
             )
             middle[at_level(l), :] = middle[at_level(l), :] + uptake_share * share
 
+        def ghost_quad(q, carry):
+            rows = pl.ds(pl.multiple_of(16 * q, 16), 16)
+            sources = [
+                arriving[step, k, rows, :].astype(jnp.float32) * ghost_mask[k, rows, :]
+                for k in range(3)
+            ]
+            blocks = [
+                jnp.where(quad_row == j, sources[k], 0.0)
+                for j in range(4)
+                for k in range(3)
+            ]
+            carried = jnp.dot(
+                jnp.concatenate(blocks, 1).astype(jnp.bfloat16),
+                ghost_tiles[pl.ds(4 * q, 4)].reshape(4 * depth, width),
+                preferred_element_type=jnp.float32,
+            )
+            for j in range(4):
+                part = carried[ROWS * (j // 2) : ROWS * (j // 2) + ROWS]
+                if j % 2:
+                    part = pltpu.roll(part, 4, 0)
+                l = 4 * q + j
+                middle[at_level(l), :] = middle[at_level(l), :] + jnp.where(
+                    upper, part, 0.0
+                )
+            return carry
+
         if step == 0:
             ghost_copy.wait()
-        for copy in copies:
-            copy.wait_recv()
-
-        def ghost_quad(q, carry):
-            rows = pl.ds(pl.multiple_of(16 * q, 16), 16)
-            source = jnp.concatenate(
-                [
-                    arriving[step, k, rows, :].astype(jnp.float32) * ghost_mask[k, rows, :]
-                    for k in range(3)
-                ],
-                1,
-            ).astype(jnp.bfloat16)
-            for j in range(4):
-                l = 4 * q + j
-                carried = jnp.dot(
-                    source, ghost_tiles[l], preferred_element_type=jnp.float32
-                )[8 * (j // 2) : 8 * (j // 2) + 8]
-                if j % 2:
-                    carried = pltpu.roll(carried, 4, 0)
-                middle[at_level(l), :] = middle[at_level(l), :] + jnp.where(
-                    upper, carried, 0.0
+        for (first, last), copies in zip(pieces, ghost_copies[step]):
+            for copy in copies:
+                copy.wait_recv()
+            lax.fori_loop(first, last, ghost_quad, 0, unroll=2)
+
+        def implicit_pairs(p, carry):
+            l = 2 * p
+            near = [middle[at_level(l + n), :] for n in range(-1, 3)]
+            settled = pair_product(near[:3], near[1:], implicit_tiles, l)
+            for n in range(2):
+                wet = (l + n).astype(jnp.float32) < wet_limit
+                fields[at_level(l + n), :] = jnp.where(
+                    wet, settled[n * ROWS : (n + 1) * ROWS], 0.0
                 )
             return carry
 
-        lax.fori_loop(0, quads, ghost_quad, 0)
-
-        if step == 0:
-            for c in range(chunks):
-                implicit_copies[c].wait()
-                lax.fori_loop(c, c + 1, implicit_chunk, 0)
-        else:
-            lax.fori_loop(0, chunks, implicit_chunk, 0)
-        for copy in copies:
-            copy.wait_send()
+        bounds = [4 * last for _, last in pieces] + [levels]
+        done, ready = 0, 0
+        for i, bound in enumerate(bounds):
+            if step == 0:
+                while ready * chunk < bound:
+                    implicit_copies[ready].wait()
+                    ready += 1
+            pairs = (bound - done) // 2
+            lax.fori_loop(
+                done // 2, bound // 2, implicit_pairs, 0, unroll=divisor(pairs, 12)
+            )
+            done = bound
+            if step < STEPS - 1 and i < len(pieces):
+                send_piece(step + 1, i)
+        for copies in ghost_copies[step]:
+            for copy in copies:
+                copy.wait_send()
 
     for l in range(levels):
         state_out[l] = fields[pl.ds((l + 1) * ROWS, tracers), :]
@@ -377,8 +414,8 @@
             pltpu.SemaphoreType.DMA((chunks,)),
             pltpu.SemaphoreType.DMA,
             pltpu.SemaphoreType.DMA((chunks,)),
-            pltpu.SemaphoreType.DMA((STEPS, 3)),
-            pltpu.SemaphoreType.DMA((STEPS, 3)),
+            pltpu.SemaphoreType.DMA((STEPS, 2, 3)),
+            pltpu.SemaphoreType.DMA((STEPS, 2, 3)),
             pltpu.SemaphoreType.DMA((tile_count,)),
             pltpu.SemaphoreType.DMA((tile_count,)),
         ],

time: 33.3 us -> 28.3 us (0.85)
  Pallas kernels: 28.2 us -> 23.1 us
    pallas_call x1, Pallas kernels: 28.2 us -> 23.1 us  [on_device(): pl.pallas_call(kernel, out_shape=(jax.ShapeDtypeStruct((levels, tracers,...]
where the time goes in v3:
time: 28.3 us; the launch traced here: 28 us
  Pallas kernels  23.1 us (82%)
  local copies, waits for them, and re-layouts  4.2 us (15%)
  between operations  0.64 us (2%)
    pallas_call x1, Pallas kernels, on_device(): pl.pallas_call(kernel, out_shape=(jax.ShapeDtypeStruct((levels, tracers,...  23.1 us
    unnamed x2, local copies, waits for them, and re-layouts  2.85 us
    reshape x1, local copies, waits for them, and re-layouts, on_device(): flux.reshape(-1)  1.35 us

profile of v3, /device:TPU:0, one launch (start us, length us, event | category | flops | bytes accessed | tf_op | source)
XLA Modules:
  0.0 28.0 jit_solution(13606413810169090674)
XLA Ops:
  0.6 23.1 %shard_map.112 = (f32[50,2,128]{2,1,0:T(2,128)}, f32[50,2,128]{2,1,0:T(2,128)}, f32[16,12]{1,0:T(8,128)}) custom-call(f32[50,2,128]{2,1,0:T(2,128)} %bitcast.12, f32[50,2,128]{2,1,0:T(2,128)} %bitcast.13, s32[6,50]{1,0:T(8,128)} %bitcast.16, s32[1,128]{1,0:T(1,128)} %bitcast.17, f32[1,128]{1,0:T(1,128)} %bitcast.18, f32[1,128]{1,0:T(1,128)} %bitcast.19, ...), custom_call_target="tpu_custom_call" | custom-call | tf_op jit(solution)/shard_map/pallas_call | solution.py:385
  23.8 1.3 %reshape.29 = f32[192]{0:T(256)} reshape(f32[16,12]{1,0:T(8,128)} %get-tuple-element.8) | data formatting | bytes 1536 | tf_op jit(solution)/shard_map/reshape | solution.py:436
  25.1 1.4 %copy.14 = f32[2,50,128]{2,0,1:T(2,128)} copy(f32[2,50,128]{2,0,1:T(2,128)} %bitcast.15) | data formatting | bytes 102400
  26.6 1.4 %copy.15 = f32[2,50,128]{2,0,1:T(2,128)} copy(f32[2,50,128]{2,0,1:T(2,128)} %bitcast.14) | data formatting | bytes 102400

commit v4 on v3

--- a/solution.py
+++ b/solution.py
@@ -381,7 +381,7 @@
     quads = -(-ghost_levels.shape[1] // 4)
     chunks = levels // divisor(levels, 10)
     vmem = pl.BlockSpec(memory_space=pltpu.VMEM)
-    anywhere = pl.BlockSpec(memory_space=pl.ANY)
+    hbm = pl.BlockSpec(memory_space=pltpu.HBM)
     state, tangent, flux = pl.pallas_call(
         kernel,
         out_shape=(
@@ -389,7 +389,7 @@
             jax.ShapeDtypeStruct((levels, tracers, width), jnp.float32),
             jax.ShapeDtypeStruct((tile_count, slot_count), jnp.float32),
         ),
-        in_specs=[anywhere] * 9,
+        in_specs=[hbm] * 9,
         out_specs=(vmem, vmem, vmem),
         scratch_shapes=[
             pltpu.VMEM((levels, tracers, width), jnp.float32),
@@ -420,9 +420,12 @@
             pltpu.SemaphoreType.DMA((tile_count,)),
         ],
         compiler_params=pltpu.CompilerParams(
-            collective_id=0, has_side_effects=True, vmem_limit_bytes=60 << 20
+            collective_id=0, has_side_effects=True, vmem_limit_bytes=40 << 20
         ),
     )(
+        *(
+            pltpu.with_memory_space_constraint(value, pltpu.HBM)
+            for value in (
         tracer_state.transpose(1, 0, 2),
         krylov_direction.transpose(1, 0, 2),
         explicit_columns.T,
@@ -432,6 +435,8 @@
         column_slots,
         explicit_tiles.reshape(levels, -1, width),
         implicit_tiles.reshape(levels, -1, width),
+            )
+        )
     )
     return (state.transpose(1, 0, 2), tangent.transpose(1, 0, 2), flux.reshape(-1))
 

time: 28.3 us -> 25.2 us (0.89)
  local copies, waits for them, and re-layouts: 4.2 us -> 1.89 us
  Pallas kernels: 23.1 us -> 22.5 us
    unnamed x2, local copies, waits for them, and re-layouts: 2.85 us -> 1.24 us
    reshape x1, local copies, waits for them, and re-layouts: 1.35 us -> 0.65 us  [on_device(): flux.reshape(-1)]
    pallas_call x1, Pallas kernels: 23.1 us -> 22.5 us  [on_device(): pl.pallas_call(kernel, out_shape=(jax.ShapeDtypeStruct((levels, tracers,...]
where the time goes in v4:
time: 25.2 us; the launch traced here: 25 us
  Pallas kernels  22.5 us (89%)
  local copies, waits for them, and re-layouts  1.89 us (8%)
  between operations  0.64 us (3%)
    pallas_call x1, Pallas kernels, on_device(): pl.pallas_call(kernel, out_shape=(jax.ShapeDtypeStruct((levels, tracers,...  22.5 us
    unnamed x2, local copies, waits for them, and re-layouts  1.24 us
    reshape x1, local copies, waits for them, and re-layouts, on_device(): flux.reshape(-1)  0.65 us

profile of v4, /device:TPU:0, one launch (start us, length us, event | category | flops | bytes accessed | tf_op | source)
XLA Modules:
  0.0 25.0 jit_solution(8740381956612942348)
XLA Ops:
  0.6 22.5 %shard_map.112 = (f32[50,2,128]{2,1,0:T(2,128)S(1)}, f32[50,2,128]{2,1,0:T(2,128)S(1)}, f32[16,12]{1,0:T(8,128)S(1)}) custom-call(f32[50,2,128]{2,1,0:T(2,128)} %bitcast.14, f32[50,2,128]{2,1,0:T(2,128)} %bitcast.15, s32[6,50]{1,0:T(8,128)} %bitcast.16, s32[1,128]{1,0:T(1,128)} %bitcast.17, f32[1,128]{1,0:T(1,128)} %bitcast.18, f32[1,128]{1,0:T(1,128)} %bitcast.19, ...), custom_call_target="tpu_custom_call" | custom-call | tf_op jit(solution)/shard_map/pallas_call | solution.py:385
  23.1 0.7 %reshape.29 = f32[192]{0:T(256)} reshape(f32[16,12]{1,0:T(8,128)S(1)} %get-tuple-element.8) | data formatting | bytes 1536 | tf_op jit(solution)/shard_map/reshape | solution.py:441
  23.8 0.6 %copy.14 = f32[2,50,128]{2,0,1:T(2,128)} copy(f32[2,50,128]{2,0,1:T(2,128)S(1)} %bitcast.11) | data formatting | bytes 102400
  24.4 0.6 %copy.15 = f32[2,50,128]{2,0,1:T(2,128)} copy(f32[2,50,128]{2,0,1:T(2,128)S(1)} %bitcast.10) | data formatting | bytes 102400

commit v5 on v4

--- a/solution.py
+++ b/solution.py
@@ -317,13 +317,6 @@
                 )
             return carry
 
-        if step == 0:
-            ghost_copy.wait()
-        for (first, last), copies in zip(pieces, ghost_copies[step]):
-            for copy in copies:
-                copy.wait_recv()
-            lax.fori_loop(first, last, ghost_quad, 0, unroll=2)
-
         def implicit_pairs(p, carry):
             l = 2 * p
             near = [middle[at_level(l + n), :] for n in range(-1, 3)]
@@ -335,20 +328,36 @@
                 )
             return carry
 
-        bounds = [4 * last for _, last in pieces] + [levels]
-        done, ready = 0, 0
-        for i, bound in enumerate(bounds):
-            if step == 0:
-                while ready * chunk < bound:
-                    implicit_copies[ready].wait()
-                    ready += 1
-            pairs = (bound - done) // 2
+        def settle(low, high):
+            while step == 0 and len(loaded) * chunk < high:
+                implicit_copies[len(loaded)].wait()
+                loaded.append(high)
+            pairs = (high - low) // 2
             lax.fori_loop(
-                done // 2, bound // 2, implicit_pairs, 0, unroll=divisor(pairs, 12)
-            )
-            done = bound
-            if step < STEPS - 1 and i < len(pieces):
-                send_piece(step + 1, i)
+                low // 2, high // 2, implicit_pairs, 0, unroll=divisor(pairs, 12)
+            )
+
+        loaded = []
+        split = 4 * pieces[0][1]
+        deep = 4 * quads + 2
+        if step == STEPS - 1:
+            settle(deep, levels)
+        if step == 0:
+            ghost_copy.wait()
+        for piece, (first, last) in enumerate(pieces):
+            for copy in ghost_copies[step][piece]:
+                copy.wait_recv()
+            lax.fori_loop(first, last, ghost_quad, 0, unroll=2)
+            if piece == 0:
+                settle(0, split - 2)
+        if step == STEPS - 1:
+            settle(split - 2, deep)
+        else:
+            settle(split - 2, split)
+            send_piece(step + 1, 0)
+            settle(split, 4 * quads)
+            send_piece(step + 1, 1)
+            settle(4 * quads, levels)
         for copies in ghost_copies[step]:
             for copy in copies:
                 copy.wait_send()

time: 25.2 us -> 24.8 us (0.984)
  Pallas kernels: 22.5 us -> 22.2 us
    pallas_call x1, Pallas kernels: 22.5 us -> 22.2 us  [on_device(): pl.pallas_call(kernel, out_shape=(jax.ShapeDtypeStruct((levels, tracers,...]
where the time goes in v5:
time: 24.8 us; the launch traced here: 24.7 us
  Pallas kernels  22.2 us (90%)
  local copies, waits for them, and re-layouts  1.89 us (8%)
  between operations  0.64 us (3%)
    pallas_call x1, Pallas kernels, on_device(): pl.pallas_call(kernel, out_shape=(jax.ShapeDtypeStruct((levels, tracers,...  22.2 us
    unnamed x2, local copies, waits for them, and re-layouts  1.24 us
    reshape x1, local copies, waits for them, and re-layouts, on_device(): flux.reshape(-1)  0.65 us

profile of v5, /device:TPU:0, one launch (start us, length us, event | category | flops | bytes accessed | tf_op | source)
XLA Modules:
  0.0 24.7 jit_solution(11535884670926201811)
XLA Ops:
  0.6 22.2 %shard_map.112 = (f32[50,2,128]{2,1,0:T(2,128)S(1)}, f32[50,2,128]{2,1,0:T(2,128)S(1)}, f32[16,12]{1,0:T(8,128)S(1)}) custom-call(f32[50,2,128]{2,1,0:T(2,128)} %bitcast.14, f32[50,2,128]{2,1,0:T(2,128)} %bitcast.15, s32[6,50]{1,0:T(8,128)} %bitcast.16, s32[1,128]{1,0:T(1,128)} %bitcast.17, f32[1,128]{1,0:T(1,128)} %bitcast.18, f32[1,128]{1,0:T(1,128)} %bitcast.19, ...), custom_call_target="tpu_custom_call" | custom-call | tf_op jit(solution)/shard_map/pallas_call | solution.py:394
  22.8 0.7 %reshape.29 = f32[192]{0:T(256)} reshape(f32[16,12]{1,0:T(8,128)S(1)} %get-tuple-element.8) | data formatting | bytes 1536 | tf_op jit(solution)/shard_map/reshape | solution.py:450
  23.5 0.6 %copy.14 = f32[2,50,128]{2,0,1:T(2,128)} copy(f32[2,50,128]{2,0,1:T(2,128)S(1)} %bitcast.11) | data formatting | bytes 102400
  24.1 0.6 %copy.15 = f32[2,50,128]{2,0,1:T(2,128)} copy(f32[2,50,128]{2,0,1:T(2,128)S(1)} %bitcast.10) | data formatting | bytes 102400
